TPU v7x, 32 devices: a whole 2x2x4 slice. The times are simulated.
32 devices in a mesh: dp: 16 (over z, x, core), mp: 2 (over y).
Axes of the slice: x: 2, y: 2, z: 4, core: 2. Of those that a mesh axis runs over, the one named last changes fastest.
Arguments:
- tokens: bfloat16 [512, 16384], P('dp', 'mp'), may hold values from -6 to 6
- gate_weight: bfloat16 [16384, 28672], P('mp', 'dp'), may hold values from -0.046875 to 0.046875
- up_weight: bfloat16 [16384, 28672], P('mp', 'dp'), may hold values from -0.046875 to 0.046875
- down_weight: bfloat16 [28672, 16384], P('dp', 'mp'), may hold values from -0.03125 to 0.03125
Outputs:
- mixed: bfloat16 [512, 16384], P('dp', 'mp')
All inputs are finite; a program needn't handle non-finite values.
Results may differ from a plain program's by a relative error of at most 0.0049.
Values may be sent and summed in bfloat16 or wider, within the bound.
No kernel may reach another device: no remote copies, remote signals or barrier semaphores. Data moves between devices by JAX's collectives and lax.ppermute only.
A program may use at most 192 MiB of HBM per device.

v0:
```python
import jax
import jax.numpy as jnp
from jax import lax
from jax.sharding import PartitionSpec as P


def per_device(tokens, gate_weight, up_weight, down_weight):
    width = gate_weight.shape[1]
    piece = lax.all_gather(tokens, "dp", axis=0, tiled=True)
    gate_part = jnp.dot(piece, gate_weight, preferred_element_type=jnp.float32)
    up_part = jnp.dot(piece, up_weight, preferred_element_type=jnp.float32)
    partial_both = jnp.concatenate([gate_part, up_part], axis=1)
    share = lax.psum_scatter(partial_both, "mp", scatter_dimension=0, tiled=True)
    own_rows = (jax.nn.silu(share[:, :width]) * share[:, width:]).astype(jnp.bfloat16)
    hidden = lax.all_gather(own_rows, "mp", axis=0, tiled=True)
    mixed = lax.psum_scatter(
        jnp.dot(hidden, down_weight, preferred_element_type=jnp.float32),
        "dp",
        scatter_dimension=0,
        tiled=True,
    )
    return mixed.astype(jnp.bfloat16)


def solution(mesh):
    return jax.shard_map(
        per_device,
        mesh=mesh,
        in_specs=(P("dp", "mp"), P("mp", "dp"), P("mp", "dp"), P("dp", "mp")),
        out_specs=P("dp", "mp"),
        check_vma=False,
    )
```

profile of v0, /device:TPU:0, one launch (start us, length us, event | category | flops | bytes accessed | tf_op | source)
XLA Modules:
  0.0 462.6 jit_solution(2330269825002777299)
XLA Ops:
  6.5 0.0 all-gather.3.cloned.1.call-start
  6.5 0.7 all-gather.3.cloned.1.call-update
  7.3 0.0 reduce-scatter.3.cloned.1.call-start
  7.3 79.2 %all-gather.3.cloned.1.call-done = bf16[512,8192]{1,0:T(8,128)(2,1)} async-done(((bf16[32,8192]{1,0:T(8,128)(2,1)}), bf16[512,8192]{1,0:T(8,128)(2,1)}) %all-gather.3.cloned.1.call-update) | async-done | bytes 8388624 | tf_op jit(solution)/shard_map/all_gather | solution.py:9
  86.5 0.0 copy-start
  86.5 21.3 %fusion.2 = f32[512,1792]{1,0:T(8,128)S(1)} fusion(bf16[512,8192]{1,0:T(8,128)(2,1)} %all-gather.3.cloned.1.call-done, bf16[8192,1792]{1,0:T(8,128)(2,1)} %param.6), kind=kOutput, calls=%fused_computation.4 | convolution fusion | flops 15032385536 | bytes 41418752 | tf_op jit(solution)/shard_map/dot_general | solution.py:11
  107.8 0.0 copy-done
  107.8 19.2 %fusion.1 = f32[512,1792]{1,0:T(8,128)S(1)} fusion(bf16[512,8192]{1,0:T(8,128)(2,1)S(1)} %copy-done, bf16[8192,1792]{1,0:T(8,128)(2,1)} %param.5), kind=kOutput, calls=%fused_computation.3 | convolution fusion | flops 15032385536 | bytes 41418752 | tf_op jit(solution)/shard_map/dot_general | solution.py:10
  127.0 4.0 pad_maximum_fusion
  131.1 0.0 reduce-scatter.3.cloned.1.call-update
  131.1 0.0 all-gather.5.cloned.1.call-start
  131.1 87.2 %reduce-scatter.3.cloned.1.call-done = f32[256,3584]{1,0:T(8,128)} async-done(((f32[512,3584]{1,0:T(8,128)}), f32[256,3584]{1,0:T(8,128)}) %reduce-scatter.3.cloned.1.call-update) | async-done | bytes 3670032 | tf_op jit(solution)/shard_map/reduce_scatter | solution.py:13
  218.3 3.5 fusion
  221.8 0.0 all-gather.5.cloned.1.call-update
  221.8 0.2 reduce-scatter.5.cloned.1.call-start
  222.1 30.1 %all-gather.5.cloned.1.call-done = bf16[512,1792]{1,0:T(8,128)(2,1)} async-done(((bf16[256,1792]{1,0:T(8,128)(2,1)}), bf16[512,1792]{1,0:T(8,128)(2,1)}) %all-gather.5.cloned.1.call-update) | async-done | bytes 1835024 | tf_op jit(solution)/shard_map/all_gather | solution.py:15
  252.1 24.4 %fusion.3 = f32[512,8192]{1,0:T(8,128)} fusion(bf16[512,1792]{1,0:T(8,128)(2,1)} %all-gather.5.cloned.1.call-done, bf16[1792,8192]{1,0:T(8,128)(2,1)} %param.7), kind=kOutput, calls=%fused_computation.5 | convolution fusion | flops 15032385536 | bytes 47972352 | tf_op jit(solution)/shard_map/dot_general | solution.py:17
  276.5 0.0 reduce-scatter.5.cloned.1.call-update
  276.6 177.5 %reduce-scatter.5.cloned.1.call-done = f32[32,8192]{1,0:T(8,128)} async-done(((f32[512,8192]{1,0:T(8,128)}), f32[32,8192]{1,0:T(8,128)}) %reduce-scatter.5.cloned.1.call-update) | async-done | bytes 1048592 | tf_op jit(solution)/shard_map/reduce_scatter | solution.py:16
  454.0 2.1 convert_element_type.7
Async XLA Ops:
  6.5 80.0 %all-gather.3.cloned.1.call-start = ((), (), s32[]{:S(2)}) async-start(), calls=%async_computation.2 | async-start | bytes 8912896 | tf_op jit(solution)/shard_map/all_gather | solution.py:9
  7.3 211.1 %reduce-scatter.3.cloned.1.call-start = ((), (), s32[]{:S(2)}) async-start(), calls=%async_computation.3 | async-start | bytes 11010048 | tf_op jit(solution)/shard_map/reduce_scatter | solution.py:13
  86.5 21.3 %copy-start = (bf16[512,8192]{1,0:T(8,128)(2,1)S(1)}, bf16[512,8192]{1,0:T(8,128)(2,1)}, u32[]{:S(2)}) copy-start(bf16[512,8192]{1,0:T(8,128)(2,1)} %all-gather.3.cloned.1.call-done) | copy-start | bytes 25165828
  131.1 121.1 %all-gather.5.cloned.1.call-start = ((), (), s32[]{:S(2)}) async-start(), calls=%async_computation.4 | async-start | bytes 2752512 | tf_op jit(solution)/shard_map/all_gather | solution.py:15
  221.8 232.2 %reduce-scatter.5.cloned.1.call-start = ((), (), s32[]{:S(2)}) async-start(), calls=%async_computation.5 | async-start | bytes 17825792 | tf_op jit(solution)/shard_map/reduce_scatter | solution.py:16
Sparse Core Ops, SparseCore 0:
  9.5 77.0 all-gather.2
  131.2 87.0 reduce-scatter.2
  222.0 30.1 all-gather.4
  276.7 177.2 reduce-scatter.4
where the time goes:
time: 463 us
  waiting for transfers between devices  375 us (81%)
  matrix products  64.8 us (14%)
  between operations  13.2 us (3%)
  other arithmetic  9.58 us (2%)
    reduce_scatter x1, waiting for transfers between devices, per_device(): lax.psum_scatter(jnp.dot(hidden, down_weight, preferred_element_type=jnp....  177 us
    reduce_scatter x1, waiting for transfers between devices, per_device(): lax.psum_scatter(partial_both, 'mp', scatter_dimension=0, tiled=True)  87.2 us
    all_gather x1, waiting for transfers between devices, per_device(): piece = lax.all_gather(tokens, 'dp', axis=0, tiled=True)  79.2 us
    all_gather x1, waiting for transfers between devices, per_device(): hidden = lax.all_gather(own_rows, 'mp', axis=0, tiled=True)  30.1 us
    dot_general x1, matrix products, per_device(): jnp.dot(hidden, down_weight, preferred_element_type=jnp.float32)  24.4 us
    dot_general x1, matrix products, per_device(): up_part = jnp.dot(piece, up_weight, preferred_element_type=jnp.float32)  21.3 us
    dot_general x1, matrix products, per_device(): gate_part = jnp.dot(piece, gate_weight, preferred_element_type=jnp.float32)  19.2 us
  transfers between devices with their start and end apart: 4, of which 4 were waited for; matrix products, arithmetic and copies ran while one was open for 0% of the time, Pallas kernels for 0%

commit v1 on v0

--- a/solution.py
+++ b/solution.py
@@ -6,7 +6,12 @@
 
 def per_device(tokens, gate_weight, up_weight, down_weight):
     width = gate_weight.shape[1]
-    piece = lax.all_gather(tokens, "dp", axis=0, tiled=True)
+    ring = [tokens]
+    for hop in range(15):
+        ring.append(lax.ppermute(ring[-1], "dp", [(dev, (dev + 1) % 16) for dev in range(16)]))
+    piece = jnp.roll(
+        jnp.concatenate(ring[::-1], axis=0), (lax.axis_index("dp") + 1) * ring[0].shape[0], axis=0
+    )
     gate_part = jnp.dot(piece, gate_weight, preferred_element_type=jnp.float32)
     up_part = jnp.dot(piece, up_weight, preferred_element_type=jnp.float32)
     partial_both = jnp.concatenate([gate_part, up_part], axis=1)

time: 463 us -> 602 us (1.30)
  waiting for transfers between devices: 375 us -> 465 us
  local copies, waits for them, and re-layouts: 0.01 us -> 46.7 us
    ppermute x0 -> x15, waiting for transfers between devices: none -> 171 us  [per_device(): lax.ppermute(ring[-1], 'dp', [(dev, (dev + 1) % 16) for dev in range(16)])]
    all_gather x1 -> x0, waiting for transfers between devices: 79.2 us -> none  [per_device(): piece = lax.all_gather(tokens, 'dp', axis=0, tiled=True)]
    unnamed x2 -> x65, local copies, waits for them, and re-layouts: 0.01 us -> 45.9 us
  transfers between devices with their start and end apart: 4 -> 18, of which waited for: 4 -> 18; matrix products, arithmetic and copies ran while one was open for 0% -> 0% of each run, Pallas kernels for 0% -> 0%
where the time goes in v1:
time: 602 us; the launch traced here: 601 us
  waiting for transfers between devices  465 us (77%)
  matrix products  66.7 us (11%)
  local copies, waits for them, and re-layouts  46.7 us (8%)
  between operations  13.2 us (2%)
  other arithmetic  9.57 us (2%)
    reduce_scatter x1, waiting for transfers between devices, per_device(): lax.psum_scatter(jnp.dot(hidden, down_weight, preferred_element_type=jnp....  177 us
    ppermute x15, waiting for transfers between devices, per_device(): lax.ppermute(ring[-1], 'dp', [(dev, (dev + 1) % 16) for dev in range(16)])  171 us
    reduce_scatter x1, waiting for transfers between devices, per_device(): lax.psum_scatter(partial_both, 'mp', scatter_dimension=0, tiled=True)  86.1 us
    unnamed x65, local copies, waits for them, and re-layouts  45.9 us
    all_gather x1, waiting for transfers between devices, per_device(): hidden = lax.all_gather(own_rows, 'mp', axis=0, tiled=True)  30.2 us
    dot_general x1, matrix products, per_device(): jnp.dot(hidden, down_weight, preferred_element_type=jnp.float32)  24.4 us
    dot_general x1, matrix products, per_device(): up_part = jnp.dot(piece, up_weight, preferred_element_type=jnp.float32)  21.1 us
    dot_general x1, matrix products, per_device(): gate_part = jnp.dot(piece, gate_weight, preferred_element_type=jnp.float32)  21.1 us
  transfers between devices with their start and end apart: 18, of which 18 were waited for; matrix products, arithmetic and copies ran while one was open for 0% of the time, Pallas kernels for 0%

profile of v1, /device:TPU:0, one launch (start us, length us, event | category | flops | bytes accessed | tf_op | source)
XLA Modules:
  0.0 601.5 jit_solution(12096724149333333235)
XLA Ops:
  7.0 12.1 %collective-permute-done = bf16[32,8192]{1,0:T(8,128)(2,1)S(1)} collective-permute-done((bf16[32,8192]{1,0:T(8,128)(2,1)}, bf16[32,8192]{1,0:T(8,128)(2,1)S(1)}, u32[]{:S(2)}, u32[]{:S(2)}) %collective-permute-start) | collective-permute-done | bytes 524320 | tf_op jit(solution)/shard_map/ppermute | solution.py:11
  19.1 11.3 %collective-permute-done.1 = bf16[32,8192]{1,0:T(8,128)(2,1)S(1)} collective-permute-done((bf16[32,8192]{1,0:T(8,128)(2,1)S(1)}, bf16[32,8192]{1,0:T(8,128)(2,1)S(1)}, u32[]{:S(2)}, u32[]{:S(2)}) %collective-permute-start.1) | collective-permute-done | bytes 524320 | tf_op jit(solution)/shard_map/ppermute | solution.py:11
  30.4 11.3 %collective-permute-done.2 = bf16[32,8192]{1,0:T(8,128)(2,1)S(1)} collective-permute-done((bf16[32,8192]{1,0:T(8,128)(2,1)S(1)}, bf16[32,8192]{1,0:T(8,128)(2,1)S(1)}, u32[]{:S(2)}, u32[]{:S(2)}) %collective-permute-start.2) | collective-permute-done | bytes 524320 | tf_op jit(solution)/shard_map/ppermute | solution.py:11
  41.7 11.3 %collective-permute-done.3 = bf16[32,8192]{1,0:T(8,128)(2,1)S(1)} collective-permute-done((bf16[32,8192]{1,0:T(8,128)(2,1)S(1)}, bf16[32,8192]{1,0:T(8,128)(2,1)S(1)}, u32[]{:S(2)}, u32[]{:S(2)}) %collective-permute-start.3) | collective-permute-done | bytes 524320 | tf_op jit(solution)/shard_map/ppermute | solution.py:11
  53.0 11.3 %collective-permute-done.4 = bf16[32,8192]{1,0:T(8,128)(2,1)S(1)} collective-permute-done((bf16[32,8192]{1,0:T(8,128)(2,1)S(1)}, bf16[32,8192]{1,0:T(8,128)(2,1)S(1)}, u32[]{:S(2)}, u32[]{:S(2)}) %collective-permute-start.4) | collective-permute-done | bytes 524320 | tf_op jit(solution)/shard_map/ppermute | solution.py:11
  64.3 11.3 %collective-permute-done.5 = bf16[32,8192]{1,0:T(8,128)(2,1)S(1)} collective-permute-done((bf16[32,8192]{1,0:T(8,128)(2,1)S(1)}, bf16[32,8192]{1,0:T(8,128)(2,1)S(1)}, u32[]{:S(2)}, u32[]{:S(2)}) %collective-permute-start.5) | collective-permute-done | bytes 524320 | tf_op jit(solution)/shard_map/ppermute | solution.py:11
  76.4 11.3 %collective-permute-done.6 = bf16[32,8192]{1,0:T(8,128)(2,1)S(1)} collective-permute-done((bf16[32,8192]{1,0:T(8,128)(2,1)S(1)}, bf16[32,8192]{1,0:T(8,128)(2,1)S(1)}, u32[]{:S(2)}, u32[]{:S(2)}) %collective-permute-start.6) | collective-permute-done | bytes 524320 | tf_op jit(solution)/shard_map/ppermute | solution.py:11
  88.5 11.3 %collective-permute-done.7 = bf16[32,8192]{1,0:T(8,128)(2,1)S(1)} collective-permute-done((bf16[32,8192]{1,0:T(8,128)(2,1)S(1)}, bf16[32,8192]{1,0:T(8,128)(2,1)S(1)}, u32[]{:S(2)}, u32[]{:S(2)}) %collective-permute-start.7) | collective-permute-done | bytes 524320 | tf_op jit(solution)/shard_map/ppermute | solution.py:11
  100.6 11.3 %collective-permute-done.8 = bf16[32,8192]{1,0:T(8,128)(2,1)S(1)} collective-permute-done((bf16[32,8192]{1,0:T(8,128)(2,1)S(1)}, bf16[32,8192]{1,0:T(8,128)(2,1)S(1)}, u32[]{:S(2)}, u32[]{:S(2)}) %collective-permute-start.8) | collective-permute-done | bytes 524320 | tf_op jit(solution)/shard_map/ppermute | solution.py:11
  112.7 11.3 %collective-permute-done.9 = bf16[32,8192]{1,0:T(8,128)(2,1)S(1)} collective-permute-done((bf16[32,8192]{1,0:T(8,128)(2,1)S(1)}, bf16[32,8192]{1,0:T(8,128)(2,1)S(1)}, u32[]{:S(2)}, u32[]{:S(2)}) %collective-permute-start.9) | collective-permute-done | bytes 524320 | tf_op jit(solution)/shard_map/ppermute | solution.py:11
  124.9 11.3 %collective-permute-done.10 = bf16[32,8192]{1,0:T(8,128)(2,1)S(1)} collective-permute-done((bf16[32,8192]{1,0:T(8,128)(2,1)S(1)}, bf16[32,8192]{1,0:T(8,128)(2,1)S(1)}, u32[]{:S(2)}, u32[]{:S(2)}) %collective-permute-start.10) | collective-permute-done | bytes 524320 | tf_op jit(solution)/shard_map/ppermute | solution.py:11
  137.0 11.3 %collective-permute-done.11 = bf16[32,8192]{1,0:T(8,128)(2,1)S(1)} collective-permute-done((bf16[32,8192]{1,0:T(8,128)(2,1)S(1)}, bf16[32,8192]{1,0:T(8,128)(2,1)S(1)}, u32[]{:S(2)}, u32[]{:S(2)}) %collective-permute-start.11) | collective-permute-done | bytes 524320 | tf_op jit(solution)/shard_map/ppermute | solution.py:11
  149.0 11.3 %collective-permute-done.12 = bf16[32,8192]{1,0:T(8,128)(2,1)S(1)} collective-permute-done((bf16[32,8192]{1,0:T(8,128)(2,1)S(1)}, bf16[32,8192]{1,0:T(8,128)(2,1)S(1)}, u32[]{:S(2)}, u32[]{:S(2)}) %collective-permute-start.12) | collective-permute-done | bytes 524320 | tf_op jit(solution)/shard_map/ppermute | solution.py:11
  161.1 11.4 %collective-permute-done.13 = bf16[32,8192]{1,0:T(8,128)(2,1)} collective-permute-done((bf16[32,8192]{1,0:T(8,128)(2,1)S(1)}, bf16[32,8192]{1,0:T(8,128)(2,1)}, u32[]{:S(2)}, u32[]{:S(2)}) %collective-permute-start.13) | collective-permute-done | bytes 524320 | tf_op jit(solution)/shard_map/ppermute | solution.py:11
  172.6 11.6 %collective-permute-done.14 = bf16[32,8192]{1,0:T(8,128)(2,1)} collective-permute-done((bf16[32,8192]{1,0:T(8,128)(2,1)}, bf16[32,8192]{1,0:T(8,128)(2,1)}, u32[]{:S(2)}, u32[]{:S(2)}) %collective-permute-start.14) | collective-permute-done | bytes 524320 | tf_op jit(solution)/shard_map/ppermute | solution.py:11
  224.5 21.1 %fusion.2 = f32[512,1792]{1,0:T(8,128)S(1)} fusion(bf16[8192,1792]{1,0:T(8,128)(2,1)} %param.5, bf16[1024,8192]{1,0:T(8,128)(2,1)} %constant_dynamic-update-slice_fusion, s32[]{:T(128)S(6)} %select_n.14), kind=kOutput, calls=%fused_computation.2 | convolution fusion | flops 15032385536 | bytes 41418756 | tf_op jit(solution)/shard_map/dot_general | solution.py:15
  245.6 21.1 %fusion = f32[512,1792]{1,0:T(8,128)S(1)} fusion(bf16[8192,1792]{1,0:T(8,128)(2,1)} %param.6, bf16[1024,8192]{1,0:T(8,128)(2,1)} %constant_dynamic-update-slice_fusion, s32[]{:T(128)S(6)} %select_n.14), kind=kOutput, calls=%fused_computation | convolution fusion | flops 15032385536 | bytes 41418756 | tf_op jit(solution)/shard_map/dot_general | solution.py:16
  266.8 4.0 pad_maximum_fusion
  271.0 86.1 %reduce-scatter.3.cloned.1.call-done = f32[256,3584]{1,0:T(8,128)} async-done(((f32[512,3584]{1,0:T(8,128)}), f32[256,3584]{1,0:T(8,128)}) %reduce-scatter.3.cloned.1.call-update) | async-done | bytes 3670032 | tf_op jit(solution)/shard_map/reduce_scatter | solution.py:18
  357.1 3.5 fusion.4
  360.7 30.2 %all-gather.2.cloned.1.call-done = bf16[512,1792]{1,0:T(8,128)(2,1)} async-done(((bf16[256,1792]{1,0:T(8,128)(2,1)}), bf16[512,1792]{1,0:T(8,128)(2,1)}) %all-gather.2.cloned.1.call-update) | async-done | bytes 1835024 | tf_op jit(solution)/shard_map/all_gather | solution.py:20
  390.9 24.4 %fusion.7 = f32[512,8192]{1,0:T(8,128)} fusion(bf16[512,1792]{1,0:T(8,128)(2,1)} %all-gather.2.cloned.1.call-done, bf16[1792,8192]{1,0:T(8,128)(2,1)} %param.7), kind=kOutput, calls=%fused_computation.41 | convolution fusion | flops 15032385536 | bytes 47972352 | tf_op jit(solution)/shard_map/dot_general | solution.py:22
  415.4 177.5 %reduce-scatter.5.cloned.1.call-done = f32[32,8192]{1,0:T(8,128)} async-done(((f32[512,8192]{1,0:T(8,128)}), f32[32,8192]{1,0:T(8,128)}) %reduce-scatter.5.cloned.1.call-update) | async-done | bytes 1048592 | tf_op jit(solution)/shard_map/reduce_scatter | solution.py:21
  592.9 2.1 convert_element_type.7
  (87 shorter events, 47.5 us)
Async XLA Ops:
  6.5 217.1 %copy-start = (bf16[32,8192]{1,0:T(8,128)(2,1)S(1)}, bf16[32,8192]{1,0:T(8,128)(2,1)}, u32[]{:S(2)}) copy-start(bf16[32,8192]{1,0:T(8,128)(2,1)} %param.4) | copy-start | bytes 1572868
  6.5 350.6 %reduce-scatter.3.cloned.1.call-start = ((), (), s32[]{:S(2)}) async-start(), calls=%async_computation.2 | async-start | bytes 11010048 | tf_op jit(solution)/shard_map/reduce_scatter | solution.py:18
  6.5 12.6 %collective-permute-start = (bf16[32,8192]{1,0:T(8,128)(2,1)}, bf16[32,8192]{1,0:T(8,128)(2,1)S(1)}, u32[]{:S(2)}, u32[]{:S(2)}) collective-permute-start(bf16[32,8192]{1,0:T(8,128)(2,1)} %param.4), channel_id=1, source_target_pairs={{0,2},{2,4},{4,6},{6,8},{8,10},{10,12},{12,14},{14,16},{16,18},{18... | collective-permute-start | bytes 1572872 | tf_op jit(solution)/shard_map/ppermute | solution.py:11
  19.1 11.3 %collective-permute-start.1 = (bf16[32,8192]{1,0:T(8,128)(2,1)S(1)}, bf16[32,8192]{1,0:T(8,128)(2,1)S(1)}, u32[]{:S(2)}, u32[]{:S(2)}) collective-permute-start(bf16[32,8192]{1,0:T(8,128)(2,1)S(1)} %collective-permute-done), channel_id=1, source_target_pairs={{0,2},{2,4},{4,6},{6,8},{8,10},{10,12},{12,14},{14,16},{16,18},{18... | collective-permute-start | bytes 1572872 | tf_op jit(solution)/shard_map/ppermute | solution.py:11
  30.4 11.3 %collective-permute-start.2 = (bf16[32,8192]{1,0:T(8,128)(2,1)S(1)}, bf16[32,8192]{1,0:T(8,128)(2,1)S(1)}, u32[]{:S(2)}, u32[]{:S(2)}) collective-permute-start(bf16[32,8192]{1,0:T(8,128)(2,1)S(1)} %collective-permute-done.1), channel_id=1, source_target_pairs={{0,2},{2,4},{4,6},{6,8},{8,10},{10,12},{12,14},{14,16},{16,18},{18... | collective-permute-start | bytes 1572872 | tf_op jit(solution)/shard_map/ppermute | solution.py:11
  41.7 11.3 %collective-permute-start.3 = (bf16[32,8192]{1,0:T(8,128)(2,1)S(1)}, bf16[32,8192]{1,0:T(8,128)(2,1)S(1)}, u32[]{:S(2)}, u32[]{:S(2)}) collective-permute-start(bf16[32,8192]{1,0:T(8,128)(2,1)S(1)} %collective-permute-done.2), channel_id=1, source_target_pairs={{0,2},{2,4},{4,6},{6,8},{8,10},{10,12},{12,14},{14,16},{16,18},{18... | collective-permute-start | bytes 1572872 | tf_op jit(solution)/shard_map/ppermute | solution.py:11
  53.0 11.3 %collective-permute-start.4 = (bf16[32,8192]{1,0:T(8,128)(2,1)S(1)}, bf16[32,8192]{1,0:T(8,128)(2,1)S(1)}, u32[]{:S(2)}, u32[]{:S(2)}) collective-permute-start(bf16[32,8192]{1,0:T(8,128)(2,1)S(1)} %collective-permute-done.3), channel_id=1, source_target_pairs={{0,2},{2,4},{4,6},{6,8},{8,10},{10,12},{12,14},{14,16},{16,18},{18... | collective-permute-start | bytes 1572872 | tf_op jit(solution)/shard_map/ppermute | solution.py:11
  64.3 11.3 %collective-permute-start.5 = (bf16[32,8192]{1,0:T(8,128)(2,1)S(1)}, bf16[32,8192]{1,0:T(8,128)(2,1)S(1)}, u32[]{:S(2)}, u32[]{:S(2)}) collective-permute-start(bf16[32,8192]{1,0:T(8,128)(2,1)S(1)} %collective-permute-done.4), channel_id=1, source_target_pairs={{0,2},{2,4},{4,6},{6,8},{8,10},{10,12},{12,14},{14,16},{16,18},{18... | collective-permute-start | bytes 1572872 | tf_op jit(solution)/shard_map/ppermute | solution.py:11
  76.4 11.3 %collective-permute-start.6 = (bf16[32,8192]{1,0:T(8,128)(2,1)S(1)}, bf16[32,8192]{1,0:T(8,128)(2,1)S(1)}, u32[]{:S(2)}, u32[]{:S(2)}) collective-permute-start(bf16[32,8192]{1,0:T(8,128)(2,1)S(1)} %collective-permute-done.5), channel_id=1, source_target_pairs={{0,2},{2,4},{4,6},{6,8},{8,10},{10,12},{12,14},{14,16},{16,18},{18... | collective-permute-start | bytes 1572872 | tf_op jit(solution)/shard_map/ppermute | solution.py:11
  88.5 11.3 %collective-permute-start.7 = (bf16[32,8192]{1,0:T(8,128)(2,1)S(1)}, bf16[32,8192]{1,0:T(8,128)(2,1)S(1)}, u32[]{:S(2)}, u32[]{:S(2)}) collective-permute-start(bf16[32,8192]{1,0:T(8,128)(2,1)S(1)} %collective-permute-done.6), channel_id=1, source_target_pairs={{0,2},{2,4},{4,6},{6,8},{8,10},{10,12},{12,14},{14,16},{16,18},{18... | collective-permute-start | bytes 1572872 | tf_op jit(solution)/shard_map/ppermute | solution.py:11
  100.6 11.3 %collective-permute-start.8 = (bf16[32,8192]{1,0:T(8,128)(2,1)S(1)}, bf16[32,8192]{1,0:T(8,128)(2,1)S(1)}, u32[]{:S(2)}, u32[]{:S(2)}) collective-permute-start(bf16[32,8192]{1,0:T(8,128)(2,1)S(1)} %collective-permute-done.7), channel_id=1, source_target_pairs={{0,2},{2,4},{4,6},{6,8},{8,10},{10,12},{12,14},{14,16},{16,18},{18... | collective-permute-start | bytes 1572872 | tf_op jit(solution)/shard_map/ppermute | solution.py:11
  112.7 11.3 %collective-permute-start.9 = (bf16[32,8192]{1,0:T(8,128)(2,1)S(1)}, bf16[32,8192]{1,0:T(8,128)(2,1)S(1)}, u32[]{:S(2)}, u32[]{:S(2)}) collective-permute-start(bf16[32,8192]{1,0:T(8,128)(2,1)S(1)} %collective-permute-done.8), channel_id=1, source_target_pairs={{0,2},{2,4},{4,6},{6,8},{8,10},{10,12},{12,14},{14,16},{16,18},{18... | collective-permute-start | bytes 1572872 | tf_op jit(solution)/shard_map/ppermute | solution.py:11
  124.9 11.3 %collective-permute-start.10 = (bf16[32,8192]{1,0:T(8,128)(2,1)S(1)}, bf16[32,8192]{1,0:T(8,128)(2,1)S(1)}, u32[]{:S(2)}, u32[]{:S(2)}) collective-permute-start(bf16[32,8192]{1,0:T(8,128)(2,1)S(1)} %collective-permute-done.9), channel_id=1, source_target_pairs={{0,2},{2,4},{4,6},{6,8},{8,10},{10,12},{12,14},{14,16},{16,18},{18... | collective-permute-start | bytes 1572872 | tf_op jit(solution)/shard_map/ppermute | solution.py:11
  137.0 11.3 %collective-permute-start.11 = (bf16[32,8192]{1,0:T(8,128)(2,1)S(1)}, bf16[32,8192]{1,0:T(8,128)(2,1)S(1)}, u32[]{:S(2)}, u32[]{:S(2)}) collective-permute-start(bf16[32,8192]{1,0:T(8,128)(2,1)S(1)} %collective-permute-done.10), channel_id=1, source_target_pairs={{0,2},{2,4},{4,6},{6,8},{8,10},{10,12},{12,14},{14,16},{16,18},{18... | collective-permute-start | bytes 1572872 | tf_op jit(solution)/shard_map/ppermute | solution.py:11
  149.0 11.3 %collective-permute-start.12 = (bf16[32,8192]{1,0:T(8,128)(2,1)S(1)}, bf16[32,8192]{1,0:T(8,128)(2,1)S(1)}, u32[]{:S(2)}, u32[]{:S(2)}) collective-permute-start(bf16[32,8192]{1,0:T(8,128)(2,1)S(1)} %collective-permute-done.11), channel_id=1, source_target_pairs={{0,2},{2,4},{4,6},{6,8},{8,10},{10,12},{12,14},{14,16},{16,18},{18... | collective-permute-start | bytes 1572872 | tf_op jit(solution)/shard_map/ppermute | solution.py:11
  161.1 11.4 %collective-permute-start.13 = (bf16[32,8192]{1,0:T(8,128)(2,1)S(1)}, bf16[32,8192]{1,0:T(8,128)(2,1)}, u32[]{:S(2)}, u32[]{:S(2)}) collective-permute-start(bf16[32,8192]{1,0:T(8,128)(2,1)S(1)} %collective-permute-done.12), channel_id=1, source_target_pairs={{0,2},{2,4},{4,6},{6,8},{8,10},{10,12},{12,14},{14,16},{16,18},{18... | collective-permute-start | bytes 1572872 | tf_op jit(solution)/shard_map/ppermute | solution.py:11
  172.6 11.6 %collective-permute-start.14 = (bf16[32,8192]{1,0:T(8,128)(2,1)}, bf16[32,8192]{1,0:T(8,128)(2,1)}, u32[]{:S(2)}, u32[]{:S(2)}) collective-permute-start(bf16[32,8192]{1,0:T(8,128)(2,1)} %collective-permute-done.13), channel_id=1, source_target_pairs={{0,2},{2,4},{4,6},{6,8},{8,10},{10,12},{12,14},{14,16},{16,18},{18... | collective-permute-start | bytes 1572872 | tf_op jit(solution)/shard_map/ppermute | solution.py:11
  172.6 42.7 %copy-start.10 = (bf16[32,8192]{1,0:T(8,128)(2,1)S(1)}, bf16[32,8192]{1,0:T(8,128)(2,1)}, u32[]{:S(2)}) copy-start(bf16[32,8192]{1,0:T(8,128)(2,1)} %copy-done.9) | copy-start | bytes 1572868
  172.6 43.5 %copy-start.8 = (bf16[32,8192]{1,0:T(8,128)(2,1)S(1)}, bf16[32,8192]{1,0:T(8,128)(2,1)}, u32[]{:S(2)}) copy-start(bf16[32,8192]{1,0:T(8,128)(2,1)} %copy-done.7) | copy-start | bytes 1572868
  172.6 44.4 %copy-start.6 = (bf16[32,8192]{1,0:T(8,128)(2,1)S(1)}, bf16[32,8192]{1,0:T(8,128)(2,1)}, u32[]{:S(2)}) copy-start(bf16[32,8192]{1,0:T(8,128)(2,1)} %copy-done.5) | copy-start | bytes 1572868
  172.6 45.2 %copy-start.4 = (bf16[32,8192]{1,0:T(8,128)(2,1)S(1)}, bf16[32,8192]{1,0:T(8,128)(2,1)}, u32[]{:S(2)}) copy-start(bf16[32,8192]{1,0:T(8,128)(2,1)} %copy-done.3) | copy-start | bytes 1572868
  172.6 46.1 %copy-start.2 = (bf16[32,8192]{1,0:T(8,128)(2,1)S(1)}, bf16[32,8192]{1,0:T(8,128)(2,1)}, u32[]{:S(2)}) copy-start(bf16[32,8192]{1,0:T(8,128)(2,1)} %copy-done.1) | copy-start | bytes 1572868
  270.8 120.2 %all-gather.2.cloned.1.call-start = ((), (), s32[]{:S(2)}) async-start(), calls=%async_computation.3 | async-start | bytes 2752512 | tf_op jit(solution)/shard_map/all_gather | solution.py:20
  360.6 232.2 %reduce-scatter.5.cloned.1.call-start = ((), (), s32[]{:S(2)}) async-start(), calls=%async_computation.4 | async-start | bytes 17825792 | tf_op jit(solution)/shard_map/reduce_scatter | solution.py:21
  (11 other events, 129.5 us)
Sparse Core Ops, SparseCore 0:
  270.9 86.1 reduce-scatter.2
  360.8 30.1 all-gather.1
  415.5 177.2 reduce-scatter.4
